TPU v7x, 32 devices: a whole 2x2x4 slice. The times are simulated.
32 devices in a mesh: row: 4 (over x, core), col: 8 (over z, y).
Axes of the slice: x: 2, y: 2, z: 4, core: 2. Of those that a mesh axis runs over, the one named last changes fastest.
Arguments:
- matrix: float32 [8, 512, 4, 1024], P(None, 'row', None, 'col'), as said below
Outputs:
- factored: float32 [8, 512, 4, 1024], P(None, 'row', None, 'col')
Inputs may be any that keep to these rules, and one draw needn't show every extreme that they name: `matrix`: Symmetric; an exponential covariance kernel exp(-distance / reach) between sites in three dimensions, plus a diagonal noise variance of 0.5 or more at each site, so every Schur complement taken during the factorization is positive definite.
All inputs are finite; a program needn't handle non-finite values.
Results may differ from a plain program's by a relative error of at most 0.00011.
Values sent between devices are 32-bit elements; how exact they have to be, the bound alone decides.
No kernel may reach another device: no remote copies, remote signals or barrier semaphores. Data moves between devices by JAX's collectives and lax.ppermute only.
A program may use at most 128 MiB of HBM per device.

v0:
```python
import jax
import jax.numpy as jnp
from jax import lax
from jax.sharding import PartitionSpec as P

STEPS = 8


def spread(block, axis, source):
    block = jnp.where(lax.axis_index(axis) == source, block, jnp.zeros_like(block))
    return lax.psum(block, axis)


def keep_blocks(rows_in, keep, block_size):
    blocked = rows_in.reshape(keep.shape[0], block_size, rows_in.shape[1])
    return jnp.where(keep[:, None, None], blocked, 0.0).reshape(rows_in.shape)


def pick_rows(rows_in, which, fold_ratio, block_size):
    blocked = rows_in.reshape(
        rows_in.shape[0] // (fold_ratio * block_size), fold_ratio, block_size, rows_in.shape[1]
    )
    chosen = lax.dynamic_slice_in_dim(blocked, which, 1, 1)
    return chosen.reshape(-1, rows_in.shape[1])


def product(left_rows, right_rows):
    return jnp.dot(
        left_rows, right_rows.T, precision=lax.Precision.HIGHEST, preferred_element_type=jnp.float32
    )


def finish(segment, panel_step, panel_rows, factor, row_ids, my_col, cols_dev, block_size):
    block_rows = row_ids.shape[0]
    block_count = segment.shape[1] // block_size
    blocked = segment.reshape(block_rows, block_size, block_count, block_size)
    col_here = jnp.arange(block_count, dtype=jnp.int32) * cols_dev + my_col
    below_mask = (row_ids > panel_step)[:, None, None, None]
    on_diagonal = (row_ids == panel_step)[:, None, None, None]
    written = jnp.where(
        below_mask,
        panel_rows.reshape(block_rows, block_size, 1, block_size),
        jnp.where(on_diagonal, factor[None, :, None, :], blocked),
    )
    blocked = jnp.where((col_here == panel_step)[None, None, :, None], written, blocked)
    blocked = jnp.where(on_diagonal & (col_here > panel_step)[None, None, :, None], 0.0, blocked)
    return blocked.reshape(segment.shape)


def local(matrix):
    rows_dev = lax.axis_size("row")
    cols_dev = lax.axis_size("col")
    my_row = lax.axis_index("row")
    my_col = lax.axis_index("col")
    block_rows = matrix.shape[0]
    block_size = matrix.shape[1]
    block_cols = matrix.shape[2]
    fold_ratio = cols_dev // rows_dev
    current = matrix.reshape(block_rows * block_size, block_cols * block_size)
    row_ids = jnp.arange(block_rows, dtype=jnp.int32) * rows_dev + my_row
    identity = jnp.eye(block_size, dtype=jnp.float32)
    upcoming = current[:, :block_size]
    for panel_step in range(STEPS):
        root_row = panel_step % rows_dev
        root_col = panel_step % cols_dev
        diag_first = panel_step // rows_dev * block_size
        diag_piece = upcoming[diag_first : diag_first + block_size]
        diagonal = spread(diag_piece, "row", root_row)
        factor = jnp.linalg.cholesky(diagonal)
        inverse = jax.scipy.linalg.solve_triangular(factor, identity, lower=True)
        panel_rows = keep_blocks(product(upcoming, inverse), row_ids > panel_step, block_size)
        across = spread(panel_rows, "col", root_col)
        mirrored = spread(
            pick_rows(across, my_col // rows_dev, fold_ratio, block_size), "row", my_col % rows_dev
        )
        current = finish(
            current - product(across, mirrored),
            panel_step,
            panel_rows,
            factor,
            row_ids,
            my_col,
            cols_dev,
            block_size,
        )
        next_first = (panel_step + 1) // cols_dev * block_size
        upcoming = current[:, next_first : next_first + block_size]
    return current.reshape(matrix.shape)


def solution(mesh):
    placed = (P(None, "row", None, "col"),)
    return jax.shard_map(
        local, mesh=mesh, in_specs=placed, out_specs=P(None, "row", None, "col"), check_vma=False
    )
```

profile of v0, /device:TPU:0, one launch (start us, length us, event | category | flops | bytes accessed | tf_op | source)
XLA Modules:
  0.0 1398.2 jit_solution(8074853636242637044)
XLA Ops:
  13.6 32.7 %all-reduce.25.cloned.1.call-done = f32[128,128]{0,1:T(8,128)} async-done(((f32[128,128]{0,1:T(8,128)}), f32[128,128]{0,1:T(8,128)}) %all-reduce.25.cloned.1.call-update) | async-done | bytes 65552 | tf_op jit(solution)/shard_map/psum | solution.py:11
  73.1 72.1 %all-reduce.27.cloned.1.call-done = f32[1024,128]{0,1:T(8,128)} async-done(((f32[1024,128]{0,1:T(8,128)}), f32[1024,128]{0,1:T(8,128)}) %all-reduce.27.cloned.1.call-update) | async-done | bytes 524304 | tf_op jit(solution)/shard_map/psum | solution.py:11
  148.7 31.1 %all-reduce.29.cloned.1.call-done = f32[512,128]{0,1:T(8,128)} async-done(((f32[512,128]{0,1:T(8,128)}), f32[512,128]{0,1:T(8,128)}) %all-reduce.29.cloned.1.call-update) | async-done | bytes 262160 | tf_op jit(solution)/shard_map/psum | solution.py:11
  185.0 31.1 %all-reduce.31.cloned.1.call-done = f32[128,128]{0,1:T(8,128)} async-done(((f32[128,128]{0,1:T(8,128)}), f32[128,128]{0,1:T(8,128)}) %all-reduce.31.cloned.1.call-update) | async-done | bytes 65552 | tf_op jit(solution)/shard_map/psum | solution.py:11
  244.3 71.6 %all-reduce.33.cloned.1.call-done = f32[1024,128]{0,1:T(8,128)} async-done(((f32[1024,128]{0,1:T(8,128)}), f32[1024,128]{0,1:T(8,128)}) %all-reduce.33.cloned.1.call-update) | async-done | bytes 524304 | tf_op jit(solution)/shard_map/psum | solution.py:11
  319.1 31.2 %all-reduce.35.cloned.1.call-done = f32[512,128]{0,1:T(8,128)} async-done(((f32[512,128]{0,1:T(8,128)}), f32[512,128]{0,1:T(8,128)}) %all-reduce.35.cloned.1.call-update) | async-done | bytes 262160 | tf_op jit(solution)/shard_map/psum | solution.py:11
  355.5 31.1 %all-reduce.37.cloned.1.call-done = f32[128,128]{0,1:T(8,128)} async-done(((f32[128,128]{0,1:T(8,128)}), f32[128,128]{0,1:T(8,128)}) %all-reduce.37.cloned.1.call-update) | async-done | bytes 65552 | tf_op jit(solution)/shard_map/psum | solution.py:11
  414.9 71.3 %all-reduce.39.cloned.1.call-done = f32[1024,128]{0,1:T(8,128)} async-done(((f32[1024,128]{0,1:T(8,128)}), f32[1024,128]{0,1:T(8,128)}) %all-reduce.39.cloned.1.call-update) | async-done | bytes 524304 | tf_op jit(solution)/shard_map/psum | solution.py:11
  489.6 31.1 %all-reduce.41.cloned.1.call-done = f32[512,128]{0,1:T(8,128)} async-done(((f32[512,128]{0,1:T(8,128)}), f32[512,128]{0,1:T(8,128)}) %all-reduce.41.cloned.1.call-update) | async-done | bytes 262160 | tf_op jit(solution)/shard_map/psum | solution.py:11
  526.5 31.2 %all-reduce.43.cloned.1.call-done = f32[128,128]{0,1:T(8,128)} async-done(((f32[128,128]{0,1:T(8,128)}), f32[128,128]{0,1:T(8,128)}) %all-reduce.43.cloned.1.call-update) | async-done | bytes 65552 | tf_op jit(solution)/shard_map/psum | solution.py:11
  586.6 71.8 %all-reduce.45.cloned.1.call-done = f32[1024,128]{0,1:T(8,128)} async-done(((f32[1024,128]{0,1:T(8,128)}), f32[1024,128]{0,1:T(8,128)}) %all-reduce.45.cloned.1.call-update) | async-done | bytes 524304 | tf_op jit(solution)/shard_map/psum | solution.py:11
  661.7 31.2 %all-reduce.47.cloned.1.call-done = f32[512,128]{0,1:T(8,128)} async-done(((f32[512,128]{0,1:T(8,128)}), f32[512,128]{0,1:T(8,128)}) %all-reduce.47.cloned.1.call-update) | async-done | bytes 262160 | tf_op jit(solution)/shard_map/psum | solution.py:11
  698.7 31.2 %all-reduce.49.cloned.1.call-done = f32[128,128]{0,1:T(8,128)} async-done(((f32[128,128]{0,1:T(8,128)}), f32[128,128]{0,1:T(8,128)}) %all-reduce.49.cloned.1.call-update) | async-done | bytes 65552 | tf_op jit(solution)/shard_map/psum | solution.py:11
  758.6 72.0 %all-reduce.51.cloned.1.call-done = f32[1024,128]{0,1:T(8,128)} async-done(((f32[1024,128]{0,1:T(8,128)}), f32[1024,128]{0,1:T(8,128)}) %all-reduce.51.cloned.1.call-update) | async-done | bytes 524304 | tf_op jit(solution)/shard_map/psum | solution.py:11
  834.3 30.8 %all-reduce.53.cloned.1.call-done = f32[512,128]{0,1:T(8,128)} async-done(((f32[512,128]{0,1:T(8,128)}), f32[512,128]{0,1:T(8,128)}) %all-reduce.53.cloned.1.call-update) | async-done | bytes 262160 | tf_op jit(solution)/shard_map/psum | solution.py:11
  870.2 31.1 %all-reduce.55.cloned.1.call-done = f32[128,128]{0,1:T(8,128)} async-done(((f32[128,128]{0,1:T(8,128)}), f32[128,128]{0,1:T(8,128)}) %all-reduce.55.cloned.1.call-update) | async-done | bytes 65552 | tf_op jit(solution)/shard_map/psum | solution.py:11
  929.9 71.1 %all-reduce.57.cloned.1.call-done = f32[1024,128]{0,1:T(8,128)} async-done(((f32[1024,128]{0,1:T(8,128)}), f32[1024,128]{0,1:T(8,128)}) %all-reduce.57.cloned.1.call-update) | async-done | bytes 524304 | tf_op jit(solution)/shard_map/psum | solution.py:11
  1004.2 31.2 %all-reduce.59.cloned.1.call-done = f32[512,128]{0,1:T(8,128)} async-done(((f32[512,128]{0,1:T(8,128)}), f32[512,128]{0,1:T(8,128)}) %all-reduce.59.cloned.1.call-update) | async-done | bytes 262160 | tf_op jit(solution)/shard_map/psum | solution.py:11
  1041.2 31.1 %all-reduce.61.cloned.1.call-done = f32[128,128]{0,1:T(8,128)} async-done(((f32[128,128]{0,1:T(8,128)}), f32[128,128]{0,1:T(8,128)}) %all-reduce.61.cloned.1.call-update) | async-done | bytes 65552 | tf_op jit(solution)/shard_map/psum | solution.py:11
  1101.1 72.0 %all-reduce.63.cloned.1.call-done = f32[1024,128]{0,1:T(8,128)} async-done(((f32[1024,128]{0,1:T(8,128)}), f32[1024,128]{0,1:T(8,128)}) %all-reduce.63.cloned.1.call-update) | async-done | bytes 524304 | tf_op jit(solution)/shard_map/psum | solution.py:11
  1176.6 31.1 %all-reduce.65.cloned.1.call-done = f32[512,128]{0,1:T(8,128)} async-done(((f32[512,128]{0,1:T(8,128)}), f32[512,128]{0,1:T(8,128)}) %all-reduce.65.cloned.1.call-update) | async-done | bytes 262160 | tf_op jit(solution)/shard_map/psum | solution.py:11
  1213.4 31.1 %all-reduce.67.cloned.1.call-done = f32[128,128]{0,1:T(8,128)} async-done(((f32[128,128]{0,1:T(8,128)}), f32[128,128]{0,1:T(8,128)}) %all-reduce.67.cloned.1.call-update) | async-done | bytes 65552 | tf_op jit(solution)/shard_map/psum | solution.py:11
  1273.4 71.9 %all-reduce.69.cloned.1.call-done = f32[1024,128]{0,1:T(8,128)} async-done(((f32[1024,128]{0,1:T(8,128)}), f32[1024,128]{0,1:T(8,128)}) %all-reduce.69.cloned.1.call-update) | async-done | bytes 524304 | tf_op jit(solution)/shard_map/psum | solution.py:11
  1352.5 29.2 %all-reduce.71.cloned.1.call-done = f32[512,128]{0,1:T(8,128)} async-done(((f32[512,128]{0,1:T(8,128)}), f32[512,128]{0,1:T(8,128)}) %all-reduce.71.cloned.1.call-update) | async-done | bytes 262160 | tf_op jit(solution)/shard_map/psum | solution.py:11
  (343 shorter events, 311.5 us)
Async XLA Ops:
  6.5 39.7 %all-reduce.25.cloned.1.call-start = ((), (), s32[]{:S(2)}) async-start(), calls=%async_computation | async-start | bytes 131072 | tf_op jit(solution)/shard_map/psum | solution.py:11
  12.3 133.0 %all-reduce.27.cloned.1.call-start = ((), (), s32[]{:S(2)}) async-start(), calls=%async_computation.1 | async-start | bytes 1048576 | tf_op jit(solution)/shard_map/psum | solution.py:11
  72.7 107.1 %all-reduce.29.cloned.1.call-start = ((), (), s32[]{:S(2)}) async-start(), calls=%async_computation.2 | async-start | bytes 524288 | tf_op jit(solution)/shard_map/psum | solution.py:11
  148.3 67.8 %all-reduce.31.cloned.1.call-start = ((), (), s32[]{:S(2)}) async-start(), calls=%async_computation.3 | async-start | bytes 131072 | tf_op jit(solution)/shard_map/psum | solution.py:11
  184.9 130.9 %all-reduce.33.cloned.1.call-start = ((), (), s32[]{:S(2)}) async-start(), calls=%async_computation.4 | async-start | bytes 1048576 | tf_op jit(solution)/shard_map/psum | solution.py:11
  243.3 107.0 %all-reduce.35.cloned.1.call-start = ((), (), s32[]{:S(2)}) async-start(), calls=%async_computation.5 | async-start | bytes 524288 | tf_op jit(solution)/shard_map/psum | solution.py:11
  318.9 67.7 %all-reduce.37.cloned.1.call-start = ((), (), s32[]{:S(2)}) async-start(), calls=%async_computation.6 | async-start | bytes 131072 | tf_op jit(solution)/shard_map/psum | solution.py:11
  355.4 130.8 %all-reduce.39.cloned.1.call-start = ((), (), s32[]{:S(2)}) async-start(), calls=%async_computation.7 | async-start | bytes 1048576 | tf_op jit(solution)/shard_map/psum | solution.py:11
  413.6 107.1 %all-reduce.41.cloned.1.call-start = ((), (), s32[]{:S(2)}) async-start(), calls=%async_computation.8 | async-start | bytes 524288 | tf_op jit(solution)/shard_map/psum | solution.py:11
  489.3 68.4 %all-reduce.43.cloned.1.call-start = ((), (), s32[]{:S(2)}) async-start(), calls=%async_computation.9 | async-start | bytes 131072 | tf_op jit(solution)/shard_map/psum | solution.py:11
  526.4 132.0 %all-reduce.45.cloned.1.call-start = ((), (), s32[]{:S(2)}) async-start(), calls=%async_computation.10 | async-start | bytes 1048576 | tf_op jit(solution)/shard_map/psum | solution.py:11
  585.9 107.0 %all-reduce.47.cloned.1.call-start = ((), (), s32[]{:S(2)}) async-start(), calls=%async_computation.11 | async-start | bytes 524288 | tf_op jit(solution)/shard_map/psum | solution.py:11
  661.5 68.3 %all-reduce.49.cloned.1.call-start = ((), (), s32[]{:S(2)}) async-start(), calls=%async_computation.12 | async-start | bytes 131072 | tf_op jit(solution)/shard_map/psum | solution.py:11
  698.6 132.0 %all-reduce.51.cloned.1.call-start = ((), (), s32[]{:S(2)}) async-start(), calls=%async_computation.13 | async-start | bytes 1048576 | tf_op jit(solution)/shard_map/psum | solution.py:11
  758.0 107.0 %all-reduce.53.cloned.1.call-start = ((), (), s32[]{:S(2)}) async-start(), calls=%async_computation.14 | async-start | bytes 524288 | tf_op jit(solution)/shard_map/psum | solution.py:11
  833.7 67.7 %all-reduce.55.cloned.1.call-start = ((), (), s32[]{:S(2)}) async-start(), calls=%async_computation.15 | async-start | bytes 131072 | tf_op jit(solution)/shard_map/psum | solution.py:11
  870.1 130.8 %all-reduce.57.cloned.1.call-start = ((), (), s32[]{:S(2)}) async-start(), calls=%async_computation.16 | async-start | bytes 1048576 | tf_op jit(solution)/shard_map/psum | solution.py:11
  928.4 107.0 %all-reduce.59.cloned.1.call-start = ((), (), s32[]{:S(2)}) async-start(), calls=%async_computation.17 | async-start | bytes 524288 | tf_op jit(solution)/shard_map/psum | solution.py:11
  1004.0 68.3 %all-reduce.61.cloned.1.call-start = ((), (), s32[]{:S(2)}) async-start(), calls=%async_computation.18 | async-start | bytes 131072 | tf_op jit(solution)/shard_map/psum | solution.py:11
  1041.1 132.0 %all-reduce.63.cloned.1.call-start = ((), (), s32[]{:S(2)}) async-start(), calls=%async_computation.19 | async-start | bytes 1048576 | tf_op jit(solution)/shard_map/psum | solution.py:11
  1100.5 107.1 %all-reduce.65.cloned.1.call-start = ((), (), s32[]{:S(2)}) async-start(), calls=%async_computation.20 | async-start | bytes 524288 | tf_op jit(solution)/shard_map/psum | solution.py:11
  1176.2 68.4 %all-reduce.67.cloned.1.call-start = ((), (), s32[]{:S(2)}) async-start(), calls=%async_computation.21 | async-start | bytes 131072 | tf_op jit(solution)/shard_map/psum | solution.py:11
  1213.3 132.0 %all-reduce.69.cloned.1.call-start = ((), (), s32[]{:S(2)}) async-start(), calls=%async_computation.22 | async-start | bytes 1048576 | tf_op jit(solution)/shard_map/psum | solution.py:11
  1272.7 109.0 %all-reduce.71.cloned.1.call-start = ((), (), s32[]{:S(2)}) async-start(), calls=%async_computation.23 | async-start | bytes 524288 | tf_op jit(solution)/shard_map/psum | solution.py:11
  (29 other events, 717.5 us)
Sparse Core Ops, SparseCore 0:
  12.4 33.7 all-reduce.24
  72.8 72.3 all-reduce.26
  148.4 31.2 all-reduce.28
  185.0 31.0 all-reduce.30
  243.4 72.3 all-reduce.32
  319.0 31.2 all-reduce.34
  355.5 31.0 all-reduce.36
  413.8 72.3 all-reduce.38
  489.4 31.2 all-reduce.40
  526.5 31.0 all-reduce.42
  586.0 72.4 all-reduce.44
  661.6 31.2 all-reduce.46
  698.7 31.0 all-reduce.48
  758.2 72.3 all-reduce.50
  833.8 31.2 all-reduce.52
  870.3 31.0 all-reduce.54
  928.5 72.3 all-reduce.56
  1004.1 31.2 all-reduce.58
  1041.2 31.0 all-reduce.60
  1100.7 72.3 all-reduce.62
  1176.3 31.2 all-reduce.64
  1213.4 31.0 all-reduce.66
  1272.9 72.3 all-reduce.68
  1350.4 31.2 all-reduce.70
where the time goes:
time: 1410 us; the launch traced here: 1400 us
  waiting for transfers between devices  1070 us (76%)
  other arithmetic  214 us (15%)
  local copies, waits for them, and re-layouts  56.8 us (4%)
  matrix products  37.2 us (3%)
  between operations  15.4 us (1%)
    psum x24, waiting for transfers between devices, spread(): return lax.psum(block, axis)  1070 us
    another operation x24, other arithmetic, local(): factor = jnp.linalg.cholesky(diagonal)  99.6 us
    another operation x16, other arithmetic, local(): inverse = jax.scipy.linalg.solve_triangular(factor, identity, lower=True)  84 us
    dot_general x16, matrix products, product(): jnp.dot(left_rows, right_rows.T, precision=lax.Precision.HIGHEST, preferr...  34.9 us
  transfers between devices with their start and end apart: 24, of which 24 were waited for; matrix products, arithmetic and copies ran while one was open for 1% of the time, Pallas kernels for 0%

commit v1 on v0

--- a/solution.py
+++ b/solution.py
@@ -8,7 +8,7 @@
 
 def spread(block, axis, source):
     block = jnp.where(lax.axis_index(axis) == source, block, jnp.zeros_like(block))
-    return lax.psum(block, axis)
+    return jnp.sum(lax.all_gather(block, axis), axis=0)
 
 
 def keep_blocks(rows_in, keep, block_size):

time: 1410 us -> 1100 us (0.78)
  waiting for transfers between devices: 1070 us -> 690 us
  blocking collectives: 0 us -> 49.2 us
  local copies, waits for them, and re-layouts: 56.8 us -> 84.9 us
    psum x24 -> x0, waiting for transfers between devices: 1070 us -> none  [spread(): return lax.psum(block, axis)]
    all_gather x0 -> x16, waiting for transfers between devices: none -> 690 us  [spread(): return jnp.sum(lax.all_gather(block, axis), axis=0)]
    all_gather x0 -> x8, blocking collectives: none -> 49.2 us  [spread(): return jnp.sum(lax.all_gather(block, axis), axis=0)]
    unnamed x69 -> x28, local copies, waits for them, and re-layouts: 21.1 us -> 51 us
    reduce_sum x0 -> x24, other arithmetic: none -> 18.6 us  [spread(): return jnp.sum(lax.all_gather(block, axis), axis=0)]
  transfers between devices with their start and end apart: 24 -> 16, of which waited for: 24 -> 16; matrix products, arithmetic and copies ran while one was open for 1% -> 2% of each run, Pallas kernels for 0% -> 0%
where the time goes in v1:
time: 1100 us
  waiting for transfers between devices  690 us (63%)
  other arithmetic  223 us (20%)
  local copies, waits for them, and re-layouts  84.9 us (8%)
  blocking collectives  49.2 us (4%)
  matrix products  31.8 us (3%)
  between operations  15.2 us (1%)
    all_gather x16, waiting for transfers between devices, spread(): return jnp.sum(lax.all_gather(block, axis), axis=0)  690 us
    another operation x24, other arithmetic, local(): factor = jnp.linalg.cholesky(diagonal)  99.4 us
    another operation x16, other arithmetic, local(): inverse = jax.scipy.linalg.solve_triangular(factor, identity, lower=True)  83.9 us
    unnamed x28, local copies, waits for them, and re-layouts  51 us
    all_gather x8, blocking collectives, spread(): return jnp.sum(lax.all_gather(block, axis), axis=0)  49.2 us
    dot_general x16, matrix products, product(): jnp.dot(left_rows, right_rows.T, precision=lax.Precision.HIGHEST, preferr...  29.5 us
  transfers between devices with their start and end apart: 16, of which 16 were waited for; matrix products, arithmetic and copies ran while one was open for 2% of the time, Pallas kernels for 0%

profile of v1, /device:TPU:0, one launch (start us, length us, event | category | flops | bytes accessed | tf_op | source)
XLA Modules:
  0.0 1097.1 jit_solution(17257660854374844439)
XLA Ops:
  15.7 11.7 %cholesky.134 = f32[128,128]{1,0:T(8,128)S(1)} custom-call(f32[128,128]{1,0:T(8,128)S(1)} %fusion.69), custom_call_target="Cholesky" | custom-call | tf_op jit(solution)/shard_map/jit(cholesky)/cholesky | solution.py:69
  40.7 74.4 %all-gather.49.cloned.1.call-done = f32[8192,128]{0,1:T(8,128)} async-done(((f32[1024,128]{0,1:T(8,128)}), f32[8192,128]{0,1:T(8,128)}) %all-gather.49.cloned.1.call-update) | async-done | bytes 4194320 | tf_op jit(solution)/shard_map/all_gather | solution.py:11
  124.0 14.4 %all-gather.33.cloned.1.call-done = f32[4,512,128]{2,1,0:T(8,128)} async-done(((f32[1,512,128]{2,1,0:T(8,128)}), f32[4,512,128]{2,1,0:T(8,128)}) %all-gather.33.cloned.1.call-update) | async-done | bytes 1048592 | tf_op jit(solution)/shard_map/all_gather | solution.py:11
  150.1 11.7 %cholesky.145 = f32[128,128]{1,0:T(8,128)S(1)} custom-call(f32[128,128]{1,0:T(8,128)S(1)} %fusion.67), custom_call_target="Cholesky" | custom-call | tf_op jit(solution)/shard_map/jit(cholesky)/cholesky | solution.py:69
  175.6 73.0 %all-gather.51.cloned.1.call-done = f32[8192,128]{0,1:T(8,128)} async-done(((f32[1024,128]{0,1:T(8,128)}), f32[8192,128]{0,1:T(8,128)}) %all-gather.51.cloned.1.call-update) | async-done | bytes 4194320 | tf_op jit(solution)/shard_map/all_gather | solution.py:11
  257.7 14.2 %all-gather.35.cloned.1.call-done = f32[4,512,128]{2,1,0:T(8,128)} async-done(((f32[1,512,128]{2,1,0:T(8,128)}), f32[4,512,128]{2,1,0:T(8,128)}) %all-gather.35.cloned.1.call-update) | async-done | bytes 1048592 | tf_op jit(solution)/shard_map/all_gather | solution.py:11
  283.6 11.7 %cholesky.156 = f32[128,128]{1,0:T(8,128)S(1)} custom-call(f32[128,128]{1,0:T(8,128)S(1)} %fusion.65), custom_call_target="Cholesky" | custom-call | tf_op jit(solution)/shard_map/jit(cholesky)/cholesky | solution.py:69
  308.7 73.3 %all-gather.53.cloned.1.call-done = f32[8192,128]{0,1:T(8,128)} async-done(((f32[1024,128]{0,1:T(8,128)}), f32[8192,128]{0,1:T(8,128)}) %all-gather.53.cloned.1.call-update) | async-done | bytes 4194320 | tf_op jit(solution)/shard_map/all_gather | solution.py:11
  396.5 10.6 all-gather.37.cloned.1.call-done
  419.5 11.7 %cholesky.167 = f32[128,128]{1,0:T(8,128)S(1)} custom-call(f32[128,128]{1,0:T(8,128)S(1)} %fusion.63), custom_call_target="Cholesky" | custom-call | tf_op jit(solution)/shard_map/jit(cholesky)/cholesky | solution.py:69
  446.0 73.0 %all-gather.55.cloned.1.call-done = f32[8192,128]{0,1:T(8,128)} async-done(((f32[1024,128]{0,1:T(8,128)}), f32[8192,128]{0,1:T(8,128)}) %all-gather.55.cloned.1.call-update) | async-done | bytes 4194320 | tf_op jit(solution)/shard_map/all_gather | solution.py:11
  528.1 14.2 %all-gather.39.cloned.1.call-done = f32[4,512,128]{2,1,0:T(8,128)} async-done(((f32[1,512,128]{2,1,0:T(8,128)}), f32[4,512,128]{2,1,0:T(8,128)}) %all-gather.39.cloned.1.call-update) | async-done | bytes 1048592 | tf_op jit(solution)/shard_map/all_gather | solution.py:11
  554.0 11.7 %cholesky.178 = f32[128,128]{1,0:T(8,128)S(1)} custom-call(f32[128,128]{1,0:T(8,128)S(1)} %fusion.61), custom_call_target="Cholesky" | custom-call | tf_op jit(solution)/shard_map/jit(cholesky)/cholesky | solution.py:69
  579.1 73.3 %all-gather.57.cloned.1.call-done = f32[8192,128]{0,1:T(8,128)} async-done(((f32[1024,128]{0,1:T(8,128)}), f32[8192,128]{0,1:T(8,128)}) %all-gather.57.cloned.1.call-update) | async-done | bytes 4194320 | tf_op jit(solution)/shard_map/all_gather | solution.py:11
  666.9 10.6 all-gather.41.cloned.1.call-done
  689.9 11.7 %cholesky.189 = f32[128,128]{1,0:T(8,128)S(1)} custom-call(f32[128,128]{1,0:T(8,128)S(1)} %fusion.59), custom_call_target="Cholesky" | custom-call | tf_op jit(solution)/shard_map/jit(cholesky)/cholesky | solution.py:69
  716.4 73.0 %all-gather.59.cloned.1.call-done = f32[8192,128]{0,1:T(8,128)} async-done(((f32[1024,128]{0,1:T(8,128)}), f32[8192,128]{0,1:T(8,128)}) %all-gather.59.cloned.1.call-update) | async-done | bytes 4194320 | tf_op jit(solution)/shard_map/all_gather | solution.py:11
  798.5 14.2 %all-gather.43.cloned.1.call-done = f32[4,512,128]{2,1,0:T(8,128)} async-done(((f32[1,512,128]{2,1,0:T(8,128)}), f32[4,512,128]{2,1,0:T(8,128)}) %all-gather.43.cloned.1.call-update) | async-done | bytes 1048592 | tf_op jit(solution)/shard_map/all_gather | solution.py:11
  824.4 11.7 %cholesky.200 = f32[128,128]{1,0:T(8,128)S(1)} custom-call(f32[128,128]{1,0:T(8,128)S(1)} %fusion.57), custom_call_target="Cholesky" | custom-call | tf_op jit(solution)/shard_map/jit(cholesky)/cholesky | solution.py:69
  849.7 73.3 %all-gather.61.cloned.1.call-done = f32[8192,128]{0,1:T(8,128)} async-done(((f32[1024,128]{0,1:T(8,128)}), f32[8192,128]{0,1:T(8,128)}) %all-gather.61.cloned.1.call-update) | async-done | bytes 4194320 | tf_op jit(solution)/shard_map/all_gather | solution.py:11
  932.0 14.2 %all-gather.45.cloned.1.call-done = f32[4,512,128]{2,1,0:T(8,128)} async-done(((f32[1,512,128]{2,1,0:T(8,128)}), f32[4,512,128]{2,1,0:T(8,128)}) %all-gather.45.cloned.1.call-update) | async-done | bytes 1048592 | tf_op jit(solution)/shard_map/all_gather | solution.py:11
  958.0 11.7 %cholesky.211 = f32[128,128]{1,0:T(8,128)S(1)} custom-call(f32[128,128]{1,0:T(8,128)S(1)} %fusion.55), custom_call_target="Cholesky" | custom-call | tf_op jit(solution)/shard_map/jit(cholesky)/cholesky | solution.py:69
  983.2 73.2 %all-gather.63.cloned.1.call-done = f32[8192,128]{0,1:T(8,128)} async-done(((f32[1024,128]{0,1:T(8,128)}), f32[8192,128]{0,1:T(8,128)}) %all-gather.63.cloned.1.call-update) | async-done | bytes 4194320 | tf_op jit(solution)/shard_map/all_gather | solution.py:11
  1070.6 10.9 all-gather.47.cloned.1.call-done
  (317 shorter events, 298.5 us)
Async XLA Ops:
  6.5 108.6 %all-gather.49.cloned.1.call-start = ((), (), s32[]{:S(2)}) async-start(), calls=%async_computation.8 | async-start | bytes 4718592 | tf_op jit(solution)/shard_map/all_gather | solution.py:11
  40.3 98.0 %all-gather.33.cloned.1.call-start = ((), (), s32[]{:S(2)}) async-start(), calls=%async_computation | async-start | bytes 1310720 | tf_op jit(solution)/shard_map/all_gather | solution.py:11
  123.2 125.4 %all-gather.51.cloned.1.call-start = ((), (), s32[]{:S(2)}) async-start(), calls=%async_computation.9 | async-start | bytes 4718592 | tf_op jit(solution)/shard_map/all_gather | solution.py:11
  139.7 1.6 copy-start.8
  143.9 31.1 %copy-start.4 = (f32[1024,512]{1,0:T(8,128)}, f32[1024,512]{1,0:T(8,128)S(1)}, u32[]{:S(2)}) copy-start(f32[1024,512]{1,0:T(8,128)S(1)} %fusion.20) | copy-start | bytes 6291460
  175.1 96.8 %all-gather.35.cloned.1.call-start = ((), (), s32[]{:S(2)}) async-start(), calls=%async_computation.1 | async-start | bytes 1310720 | tf_op jit(solution)/shard_map/all_gather | solution.py:11
  256.7 125.3 %all-gather.53.cloned.1.call-start = ((), (), s32[]{:S(2)}) async-start(), calls=%async_computation.10 | async-start | bytes 4718592 | tf_op jit(solution)/shard_map/all_gather | solution.py:11
  273.2 1.6 copy-start.5
  308.5 98.6 %all-gather.37.cloned.1.call-start = ((), (), s32[]{:S(2)}) async-start(), calls=%async_computation.2 | async-start | bytes 1310720 | tf_op jit(solution)/shard_map/all_gather | solution.py:11
  391.9 127.2 %all-gather.55.cloned.1.call-start = ((), (), s32[]{:S(2)}) async-start(), calls=%async_computation.11 | async-start | bytes 4718592 | tf_op jit(solution)/shard_map/all_gather | solution.py:11
  412.0 1.3 copy-start.6
  445.5 96.8 %all-gather.39.cloned.1.call-start = ((), (), s32[]{:S(2)}) async-start(), calls=%async_computation.3 | async-start | bytes 1310720 | tf_op jit(solution)/shard_map/all_gather | solution.py:11
  527.1 125.3 %all-gather.57.cloned.1.call-start = ((), (), s32[]{:S(2)}) async-start(), calls=%async_computation.12 | async-start | bytes 4718592 | tf_op jit(solution)/shard_map/all_gather | solution.py:11
  543.6 1.6 copy-start.7
  578.9 98.6 %all-gather.41.cloned.1.call-start = ((), (), s32[]{:S(2)}) async-start(), calls=%async_computation.4 | async-start | bytes 1310720 | tf_op jit(solution)/shard_map/all_gather | solution.py:11
  662.3 127.2 %all-gather.59.cloned.1.call-start = ((), (), s32[]{:S(2)}) async-start(), calls=%async_computation.13 | async-start | bytes 4718592 | tf_op jit(solution)/shard_map/all_gather | solution.py:11
  715.9 96.8 %all-gather.43.cloned.1.call-start = ((), (), s32[]{:S(2)}) async-start(), calls=%async_computation.5 | async-start | bytes 1310720 | tf_op jit(solution)/shard_map/all_gather | solution.py:11
  797.5 125.4 %all-gather.61.cloned.1.call-start = ((), (), s32[]{:S(2)}) async-start(), calls=%async_computation.14 | async-start | bytes 4718592 | tf_op jit(solution)/shard_map/all_gather | solution.py:11
  814.0 1.6 copy-start.1
  818.3 31.1 %copy-start.2 = (f32[1024,512]{1,0:T(8,128)}, f32[1024,512]{1,0:T(8,128)S(1)}, u32[]{:S(2)}) copy-start(f32[1024,512]{1,0:T(8,128)S(1)} %fusion.5) | copy-start | bytes 6291460
  849.4 96.8 %all-gather.45.cloned.1.call-start = ((), (), s32[]{:S(2)}) async-start(), calls=%async_computation.6 | async-start | bytes 1310720 | tf_op jit(solution)/shard_map/all_gather | solution.py:11
  931.0 125.4 %all-gather.63.cloned.1.call-start = ((), (), s32[]{:S(2)}) async-start(), calls=%async_computation.15 | async-start | bytes 4718592 | tf_op jit(solution)/shard_map/all_gather | solution.py:11
  947.5 1.6 copy-start.3
  982.8 98.6 %all-gather.47.cloned.1.call-start = ((), (), s32[]{:S(2)}) async-start(), calls=%async_computation.7 | async-start | bytes 1310720 | tf_op jit(solution)/shard_map/all_gather | solution.py:11
  (1 other events, 1.3 us)
Sparse Core Ops, SparseCore 0:
  40.4 74.6 all-gather.48
  123.3 14.9 all-gather.32
  175.2 73.4 all-gather.50
  256.9 14.9 all-gather.34
  308.6 73.3 all-gather.52
  392.0 14.9 all-gather.36
  445.6 73.3 all-gather.54
  527.3 14.9 all-gather.38
  579.0 73.4 all-gather.56
  662.4 14.9 all-gather.40
  716.0 73.4 all-gather.58
  797.7 14.9 all-gather.42
  849.5 73.4 all-gather.60
  931.2 14.9 all-gather.44
  983.0 73.4 all-gather.62
  1066.4 14.9 all-gather.46
